TPU v7x, 512 devices: a whole 4x4x16 slice. The times are simulated.
512 devices in a mesh: ctx: 64 (over x, z), head: 8 (over y, core).
Axes of the slice: x: 4, y: 4, z: 16, core: 2. Of those that a mesh axis runs over, the one named last changes fastest.
Arguments:
- prefix_len: int32 [2], replicated, may hold values from 2048 to 16384, as said below
- page_slot: int32 [2, 64], replicated, may hold values from 0 to 127, as said below
- queries: bfloat16 [512, 8192], P('ctx', 'head'), may hold values from -6 to 6
- new_kv: bfloat16 [2, 512, 1024], P(None, 'ctx', 'head'), may hold values from -6 to 6
- cache: bfloat16 [2, 128, 256, 1024], P(None, 'ctx', None, 'head'), may hold values from -6 to 6
Outputs:
- attention: bfloat16 [512, 8192], P(('ctx', 'head'))
Inputs may be any that keep to these rules, and one draw needn't show every extreme that they name: `prefix_len`: each conversation's prefix holds 2048 to 16384 tokens; one conversation holds exactly 16384. `page_slot`: every slot number appears once; slot s lies at ctx index s // 2, as its slot s % 2.
All inputs are finite; a program needn't handle non-finite values.
Results may differ from a plain program's by a relative error of at most 0.0075.
Values may be sent and summed in bfloat16 or wider, within the bound.
A program may use at most 64 MiB of HBM per device.

v0:
```python
import jax
import jax.numpy as jnp
from jax import lax
from jax.sharding import PartitionSpec as P

HEAD_DIM = 128
SPAN = 256
PAGE = 256
MAXPAGES = 64
MASKED = -1e30


def slot_owners(page_slot, first_slot, slot_count):
    flat_table = page_slot.reshape(-1)
    wanted = first_slot + jnp.arange(slot_count, dtype=jnp.int32)
    matches = (flat_table[None, :] == wanted[:, None]).astype(jnp.int32)
    item_ids = jnp.arange(flat_table.shape[0], dtype=jnp.int32)
    return jnp.sum(matches * item_ids[None, :], axis=1)


def raise_rows(row_max, row_start, candidate):
    previous = lax.dynamic_slice_in_dim(row_max, row_start, candidate.shape[0], 0)
    return lax.dynamic_update_slice_in_dim(row_max, jnp.maximum(previous, candidate), row_start, 0)


def add_rows(totals, row_start, term):
    previous = lax.dynamic_slice_in_dim(totals, row_start, term.shape[0], 0)
    return lax.dynamic_update_slice_in_dim(totals, previous + term, row_start, 0)


def weigh_scores(scores, row_top):
    return jnp.exp(scores - row_top[..., None]).astype(jnp.bfloat16)


def local(prefix_len, page_slot, queries, new_kv, cache):
    own_rows = queries.shape[0]
    kv_local = new_kv.shape[2] // HEAD_DIM
    group_size = queries.shape[1] // HEAD_DIM // kv_local
    slot_count = cache.shape[1]
    score_scale = HEAD_DIM ** (-0.5)
    ctx_place = lax.axis_index("ctx")
    gathered = lax.all_gather(queries, "ctx", axis=0, tiled=True)
    total_rows = gathered.shape[0]
    gathered = gathered.reshape(total_rows, kv_local, group_size, HEAD_DIM)
    slot_items = slot_owners(page_slot, ctx_place * slot_count, slot_count)
    slot_dialog = slot_items // MAXPAGES
    slot_page = slot_items % MAXPAGES
    dialog_ids = jnp.arange(prefix_len.shape[0], dtype=jnp.int32)
    slot_length = jnp.sum(
        (dialog_ids[None, :] == slot_dialog[:, None]).astype(jnp.int32) * prefix_len[None, :],
        axis=1,
    )
    key_pages = cache[0].reshape(slot_count, PAGE, kv_local, HEAD_DIM)
    value_pages = cache[1].reshape(slot_count, PAGE, kv_local, HEAD_DIM)
    offsets = jnp.arange(PAGE, dtype=jnp.int32)

    def slot_start(slot_index):
        return slot_dialog[slot_index] * SPAN

    def slot_scores(slot_index):
        query_rows = lax.dynamic_slice_in_dim(gathered, slot_start(slot_index), SPAN, 0)
        page_keys = lax.dynamic_index_in_dim(key_pages, slot_index, 0, keepdims=False)
        raw_scores = (
            jnp.einsum("tghd,pgd->tghp", query_rows, page_keys, preferred_element_type=jnp.float32)
            * score_scale
        )
        live_keys = slot_page[slot_index] * PAGE + offsets < slot_length[slot_index]
        return jnp.where(live_keys, raw_scores, MASKED)

    def max_step(slot_index, row_max):
        return raise_rows(row_max, slot_start(slot_index), jnp.max(slot_scores(slot_index), axis=3))

    row_max = jnp.full((total_rows, kv_local, group_size), MASKED, jnp.float32)
    row_max = lax.fori_loop(0, slot_count, max_step, row_max)
    own_start = ctx_place * own_rows
    own_dialog_start = own_start // SPAN * SPAN
    own_offset = own_start % SPAN
    turn_steps = jnp.arange(SPAN, dtype=jnp.int32)
    own_steps = own_offset + jnp.arange(own_rows, dtype=jnp.int32)
    own_kv = new_kv.reshape(2, own_rows, kv_local, HEAD_DIM)
    dialog_queries = lax.dynamic_slice_in_dim(gathered, own_dialog_start, SPAN, 0)
    self_raw = (
        jnp.einsum("tghd,pgd->tghp", dialog_queries, own_kv[0], preferred_element_type=jnp.float32)
        * score_scale
    )
    causal = own_steps[None, :] <= turn_steps[:, None]
    self_scores = jnp.where(causal[:, None, None, :], self_raw, MASKED)
    self_values = own_kv[1]
    row_max = raise_rows(row_max, own_dialog_start, jnp.max(self_scores, axis=3))
    row_max = lax.pmax(row_max, "ctx")

    def slot_weights(slot_index):
        row_top = lax.dynamic_slice_in_dim(row_max, slot_start(slot_index), SPAN, 0)
        return weigh_scores(slot_scores(slot_index), row_top)

    def slot_values(slot_index, weights):
        page_values = lax.dynamic_index_in_dim(value_pages, slot_index, 0, keepdims=False)
        return jnp.einsum(
            "tghp,pgd->tghd", weights, page_values, preferred_element_type=jnp.float32
        )

    self_top = lax.dynamic_slice_in_dim(row_max, own_dialog_start, self_scores.shape[0], 0)
    self_weights = weigh_scores(self_scores, self_top)
    self_term = jnp.einsum(
        "tghp,pgd->tghd", self_weights, self_values, preferred_element_type=jnp.float32
    )
    self_sum = jnp.sum(self_weights.astype(jnp.float32), axis=3)
    weight_sums = jnp.zeros((total_rows, kv_local, group_size), jnp.float32)

    def sum_step(slot_index, carried):
        value_sums, weight_sums = carried
        row_start = slot_start(slot_index)
        weights = slot_weights(slot_index)
        return (
            add_rows(value_sums, row_start, slot_values(slot_index, weights)),
            add_rows(weight_sums, row_start, jnp.sum(weights.astype(jnp.float32), axis=3)),
        )

    value_sums = jnp.zeros((total_rows, kv_local, group_size, HEAD_DIM), jnp.float32)
    value_sums, weight_sums = lax.fori_loop(0, slot_count, sum_step, (value_sums, weight_sums))
    value_sums = add_rows(value_sums, own_dialog_start, self_term)
    own_sums = lax.psum_scatter(value_sums, "ctx", scatter_dimension=0, tiled=True)
    weight_sums = add_rows(weight_sums, own_dialog_start, self_sum)
    all_weights = lax.psum(weight_sums, "ctx")
    own_weights = lax.dynamic_slice_in_dim(all_weights, own_start, own_rows, 0)
    attention = (own_sums / own_weights[..., None]).astype(jnp.bfloat16)
    attention = attention.reshape(own_rows, kv_local * group_size * HEAD_DIM)
    return lax.all_to_all(attention, "head", split_axis=0, concat_axis=1, tiled=True)


def solution(mesh):
    return jax.shard_map(
        local,
        mesh=mesh,
        in_specs=(P(), P(), P("ctx", "head"), P(None, "ctx", "head"), P(None, "ctx", None, "head")),
        out_specs=P(("ctx", "head"), None),
        check_vma=False,
    )
```

profile of v0, /device:TPU:1, one launch (start us, length us, event | category | flops | bytes accessed | tf_op | source)
XLA Modules:
  0.0 1162.4 jit_solution(1225460248893137209)
XLA Ops:
  6.5 0.7 all-gather.2.cloned.1.call-update
  7.3 0.8 eq.32
  8.1 1.0 slice_bitcast_fusion
  9.4 0.8 fusion.41
  10.3 134.7 %all-gather.2.cloned.1.call-done = bf16[512,1024]{1,0:T(8,128)(2,1)} async-done(((bf16[8,1024]{1,0:T(8,128)(2,1)}), bf16[512,1024]{1,0:T(8,128)(2,1)}) %all-gather.2.cloned.1.call-update) | async-done | bytes 1048592 | tf_op jit(solution)/shard_map/all_gather | solution.py:42
  145.1 1.5 copy.40
  147.3 8.8 while.30
  150.5 0.7 fusion.55
  154.8 0.7 fusion.55
  156.3 222.5 %pmax.7 = f32[512,1,8]{0,2,1:T(8,128)S(1)} all-reduce(f32[512,1,8]{0,2,1:T(8,128)S(1)} %fusion.34), channel_id=1, replica_groups=mesh['ctx'=64,'head'=8] {'ctx'}, use_global_device_ids=true, to_apply=%region_6.7 | all-reduce | flops 4096 | bytes 32768 | tf_op jit(solution)/shard_map/pmax | solution.py:90
  379.1 10.0 while.31
  382.3 0.7 fusion.60
  386.6 0.7 dynamic_slice.215
  387.2 0.7 fusion.60
  389.0 1.8 copy.44
  390.8 1.9 copy.45
  392.7 1.7 fusion.28
  394.6 0.7 copy_dynamic-update-slice_fusion
  395.3 1.3 copy-done.1
  397.0 218.9 %psum.7 = f32[512,1,8]{2,0,1:T(8,128)S(1)} all-reduce(f32[512,1,8]{2,0,1:T(8,128)S(1)} %constant_dynamic-update-slice_fusion), channel_id=1, replica_groups=mesh['ctx'=64,'head'=8] {'ctx'}, use_global_device_ids=true, to_apply=%region_12.13 | all-reduce | flops 4096 | bytes 32768 | tf_op jit(solution)/shard_map/psum | solution.py:124
  615.9 516.2 %reduce-scatter.2.cloned.1.call-done = f32[8,1,8,128]{3,2,1,0:T(8,128)} async-done(((f32[512,1,8,128]{3,2,1,0:T(8,128)}), f32[8,1,8,128]{3,2,1,0:T(8,128)}) %reduce-scatter.2.cloned.1.call-update) | async-done | bytes 32784 | tf_op jit(solution)/shard_map/reduce_scatter | solution.py:122
  1132.1 0.8 divide_convert_fusion
  1133.5 0.7 reduce.9
  1134.3 20.6 %all_to_all.17 = bf16[8,2,512]{2,1,0:T(2,128)(2,1)S(1)} all-to-all(bf16[8,2,512]{2,1,0:T(2,128)(2,1)S(1)} %reshape.169), channel_id=1, replica_groups=mesh['ctx'=64,'head'=8] {'head'}, dimensions={0} | all-to-all | bytes 32768 | tf_op jit(solution)/shard_map/all_to_all | solution.py:128
  (54 shorter events, 13.2 us)
Async XLA Ops:
  6.5 138.5 %all-gather.2.cloned.1.call-start = ((), (), s32[]{:S(2)}) async-start(), calls=%async_computation.2 | async-start | bytes 1064960 | tf_op jit(solution)/shard_map/all_gather | solution.py:42
  7.3 1124.9 %reduce-scatter.2.cloned.1.call-start = ((), (), s32[]{:S(2)}) async-start(), calls=%async_computation.3 | async-start | bytes 2129920 | tf_op jit(solution)/shard_map/reduce_scatter | solution.py:122
  147.2 8.8 copy-start.2
  392.7 1.9 copy-start
  395.3 1.4 copy-start.1
Sparse Core Ops, SparseCore 0:
  10.3 134.7 all-gather.1
  396.8 735.2 reduce-scatter.1
where the time goes:
time: 1160 us
  waiting for transfers between devices  652 us (56%)
  blocking collectives  462 us (40%)
  local copies, waits for them, and re-layouts  19.3 us (2%)
  between operations  13.6 us (1%)
    reduce_scatter x1, waiting for transfers between devices, local(): lax.psum_scatter(value_sums, 'ctx', scatter_dimension=0, tiled=True)  516 us
    pmax x1, blocking collectives, local(): row_max = lax.pmax(row_max, 'ctx')  223 us
    psum x1, blocking collectives, local(): all_weights = lax.psum(weight_sums, 'ctx')  219 us
    all_gather x1, waiting for transfers between devices, local(): gathered = lax.all_gather(queries, 'ctx', axis=0, tiled=True)  135 us
  transfers between devices with their start and end apart: 2, of which 2 were waited for; matrix products, arithmetic and copies ran while one was open for 0% of the time, Pallas kernels for 0%

commit v1 on v0

--- a/solution.py
+++ b/solution.py
@@ -8,6 +8,11 @@
 PAGE = 256
 MAXPAGES = 64
 MASKED = -1e30
+
+
+def gather_over(array, axis, along):
+    sent = jnp.stack([array] * lax.axis_size(axis))
+    return jnp.concatenate(lax.all_to_all(sent, axis, 0, 0), axis=along)
 
 
 def slot_owners(page_slot, first_slot, slot_count):
@@ -39,7 +44,7 @@
     slot_count = cache.shape[1]
     score_scale = HEAD_DIM ** (-0.5)
     ctx_place = lax.axis_index("ctx")
-    gathered = lax.all_gather(queries, "ctx", axis=0, tiled=True)
+    gathered = gather_over(queries, "ctx", 0)
     total_rows = gathered.shape[0]
     gathered = gathered.reshape(total_rows, kv_local, group_size, HEAD_DIM)
     slot_items = slot_owners(page_slot, ctx_place * slot_count, slot_count)

time: 1160 us -> 1090 us (0.940)
  waiting for transfers between devices: 652 us -> 558 us
  starting transfers between devices: 0.04 us -> 19.2 us
    all_gather x1 -> x0, waiting for transfers between devices: 135 us -> none  [local(): gathered = lax.all_gather(queries, 'ctx', axis=0, tiled=True)]
    all_to_all x0 -> x1, waiting for transfers between devices: none -> 49.5 us  [gather_over(): return jnp.concatenate(lax.all_to_all(sent, axis, 0, 0), axis=along)]
    all_to_all x0 -> x1, starting transfers between devices: none -> 19.1 us  [gather_over(): return jnp.concatenate(lax.all_to_all(sent, axis, 0, 0), axis=along)]
where the time goes in v1:
time: 1090 us
  waiting for transfers between devices  558 us (51%)
  blocking collectives  462 us (42%)
  starting transfers between devices  19.2 us (2%)
  local copies, waits for them, and re-layouts  17.8 us (2%)
  between operations  13.7 us (1%)
    reduce_scatter x1, waiting for transfers between devices, local(): lax.psum_scatter(value_sums, 'ctx', scatter_dimension=0, tiled=True)  509 us
    pmax x1, blocking collectives, local(): row_max = lax.pmax(row_max, 'ctx')  222 us
    psum x1, blocking collectives, local(): all_weights = lax.psum(weight_sums, 'ctx')  219 us
    all_to_all x1, waiting for transfers between devices, gather_over(): return jnp.concatenate(lax.all_to_all(sent, axis, 0, 0), axis=along)  49.5 us
  transfers between devices with their start and end apart: 2, of which 2 were waited for; matrix products, arithmetic and copies ran while one was open for 0% of the time, Pallas kernels for 0%

profile of v1, /device:TPU:1, one launch (start us, length us, event | category | flops | bytes accessed | tf_op | source)
XLA Modules:
  0.0 1086.1 jit_solution(3473644442290407952)
XLA Ops:
  6.5 1.9 stack.2
  8.4 19.1 %all-to-all-start = ((bf16[64,8,1024]{2,1,0:T(8,128)(2,1)}), bf16[64,8,1024]{2,1,0:T(8,128)(2,1)S(1)}, u32[]{:S(2)}, u32[]{:S(2)}) async-start(bf16[64,8,1024]{2,1,0:T(8,128)(2,1)} %stack.2), calls=%async_computation | async-start | bytes 2097152 | tf_op jit(solution)/shard_map/all_to_all | solution.py:15
  28.4 49.5 %all-to-all-done = bf16[64,8,1024]{2,1,0:T(8,128)(2,1)S(1)} async-done(((bf16[64,8,1024]{2,1,0:T(8,128)(2,1)}), bf16[64,8,1024]{2,1,0:T(8,128)(2,1)S(1)}, u32[]{:S(2)}, u32[]{:S(2)}) %all-to-all-start) | async-done | bytes 1048608 | tf_op jit(solution)/shard_map/all_to_all | solution.py:15
  78.3 8.7 while.30
  79.7 0.7 dynamic_slice.201
  81.5 0.7 fusion.54
  84.0 0.7 dynamic_slice.201
  85.9 0.7 fusion.54
  87.4 222.3 %pmax.7 = f32[512,1,8]{0,2,1:T(8,128)S(1)} all-reduce(f32[512,1,8]{0,2,1:T(8,128)S(1)} %fusion.34), channel_id=1, replica_groups=mesh['ctx'=64,'head'=8] {'ctx'}, use_global_device_ids=true, to_apply=%region_6.7 | all-reduce | flops 4096 | bytes 32768 | tf_op jit(solution)/shard_map/pmax | solution.py:95
  309.9 9.9 while.31
  311.3 0.7 dynamic_slice.210
  313.1 0.7 fusion.59
  316.3 0.7 dynamic_slice.210
  318.1 0.7 fusion.59
  319.9 1.9 copy.42
  321.8 1.8 copy.41
  323.6 1.7 fusion.28
  325.5 0.7 copy_dynamic-update-slice_fusion
  326.2 1.3 copy-done.1
  327.9 219.0 %psum.7 = f32[512,1,8]{2,0,1:T(8,128)S(1)} all-reduce(f32[512,1,8]{2,0,1:T(8,128)S(1)} %constant_dynamic-update-slice_fusion), channel_id=1, replica_groups=mesh['ctx'=64,'head'=8] {'ctx'}, use_global_device_ids=true, to_apply=%region_12.13 | all-reduce | flops 4096 | bytes 32768 | tf_op jit(solution)/shard_map/psum | solution.py:129
  546.9 508.8 %reduce-scatter.2.cloned.1.call-done = f32[8,1,8,128]{3,2,1,0:T(8,128)} async-done(((f32[512,1,8,128]{3,2,1,0:T(8,128)}), f32[8,1,8,128]{3,2,1,0:T(8,128)}) %reduce-scatter.2.cloned.1.call-update) | async-done | bytes 32784 | tf_op jit(solution)/shard_map/reduce_scatter | solution.py:127
  1055.8 0.8 divide_convert_fusion
  1057.2 0.7 reduce.9
  1057.9 20.7 %all_to_all.22 = bf16[8,2,512]{2,1,0:T(2,128)(2,1)S(1)} all-to-all(bf16[8,2,512]{2,1,0:T(2,128)(2,1)S(1)} %reshape.167), channel_id=1, replica_groups=mesh['ctx'=64,'head'=8] {'head'}, dimensions={0} | all-to-all | bytes 32768 | tf_op jit(solution)/shard_map/all_to_all | solution.py:133
  (61 shorter events, 11.4 us)
Async XLA Ops:
  6.5 21.1 %copy-start.4 = (s32[2,64]{1,0:T(2,128)S(1)}, s32[2,64]{1,0:T(2,128)}, u32[]{:S(2)}) copy-start(s32[2,64]{1,0:T(2,128)} %param.10) | copy-start | bytes 1540
  6.5 21.2 %copy-start.2 = (bf16[2,2,256,128]{3,2,1,0:T(8,128)(2,1)S(1)}, bf16[2,2,256,128]{3,2,1,0:T(8,128)(2,1)}, u32[]{:S(2)}) copy-start(bf16[2,2,256,128]{3,2,1,0:T(8,128)(2,1)} %param.13) | copy-start | bytes 786436
  6.5 21.6 %copy-start.5 = (s32[2]{0:T(128)S(1)}, s32[2]{0:T(128)}, u32[]{:S(2)}) copy-start(s32[2]{0:T(128)} %param.9) | copy-start | bytes 28
  8.4 69.4 %all-to-all-start = ((bf16[64,8,1024]{2,1,0:T(8,128)(2,1)}), bf16[64,8,1024]{2,1,0:T(8,128)(2,1)S(1)}, u32[]{:S(2)}, u32[]{:S(2)}) async-start(bf16[64,8,1024]{2,1,0:T(8,128)(2,1)} %stack.2), calls=%async_computation | async-start | bytes 2097152 | tf_op jit(solution)/shard_map/all_to_all | solution.py:15
  27.5 1028.2 %reduce-scatter.2.cloned.1.call-start = ((), (), s32[]{:S(2)}) async-start(), calls=%async_computation.3 | async-start | bytes 2129920 | tf_op jit(solution)/shard_map/reduce_scatter | solution.py:127
  78.3 8.8 copy-start.3
  323.6 1.9 copy-start
  326.2 1.4 copy-start.1
Sparse Core Ops, SparseCore 0:
  327.7 728.0 reduce-scatter.1
